TPU v7x, 128 devices: a whole 4x4x4 slice. The times are simulated.
128 devices in a mesh: grp: 8 (over z, core), sub: 16 (over y, x).
Axes of the slice: x: 4, y: 4, z: 4, core: 2. Of those that a mesh axis runs over, the one named last changes fastest.
Arguments:
- activations: bfloat16 [196608, 2048], P(('grp', 'sub')), may hold values from -16 to 16, as said below
- cotangent: bfloat16 [196608, 1024], P(('grp', 'sub')), may hold values from -16 to 16, as said below
- weight: bfloat16 [2048, 1024], replicated, may hold values from -0.125 to 0.125
- master: float32 [2048, 1024], P(('grp', 'sub')), may hold values from -1.5 to 1.5
- momentum: float32 [2048, 1024], P(('grp', 'sub')), may hold values from -6 to 6
Outputs:
- input_grad: bfloat16 [196608, 2048], P(('grp', 'sub'))
- new_momentum: float32 [2048, 1024], P(('grp', 'sub'))
- new_master: float32 [2048, 1024], P(('grp', 'sub'))
- new_weight: bfloat16 [2048, 1024], replicated
Inputs may be any that keep to these rules, and one draw needn't show every extreme that they name: `activations`: activations of the kind a projection receives. `cotangent`: gradients of the kind a loss gives.
All inputs are finite; a program needn't handle non-finite values.
Results may differ from a plain program's by a relative error of at most 0.001.
Values may be sent and summed in bfloat16 or wider, within the bound.
A program may use at most 128 MiB of HBM per device.

v0:
```python
import math

import jax
import jax.numpy as jnp
from jax import lax
from jax.sharding import PartitionSpec as P


def partner(value, axis, distance):
    mask = 2**distance
    pairs = [(source, source ^ mask) for source in range(lax.axis_size(axis))]
    return lax.ppermute(value, axis, pairs)


def node_sums(partial_value, level):
    totals = lax.psum(partial_value, "sub")
    for bit_pos in range(level + 1):
        totals = totals + partner(totals, "grp", bit_pos)
    return totals


def adasum_pair(lower, upper, totals):
    lower_sq = totals[0]
    upper_sq = totals[1]
    cross = totals[2]
    return (1.0 - cross / (2.0 * (lower_sq + 1e-06))) * lower + (
        1.0 - cross / (2.0 * (upper_sq + 1e-06))
    ) * upper


def body(activations, cotangent, weight, master, momentum):
    n_grp = lax.axis_size("grp")
    n_sub = lax.axis_size("sub")
    rows, width = activations.shape
    kv_width = cotangent.shape[1]
    block = width // (n_grp * n_sub)
    scale = 1.0 / math.sqrt(rows * n_sub)
    input_grad = lax.dot_general(
        cotangent, weight, (((1,), (1,)), ((), ())), preferred_element_type=jnp.float32
    ).astype(jnp.bfloat16)
    product = lax.dot_general(
        activations, cotangent, (((0,), (0,)), ((), ())), preferred_element_type=jnp.float32
    )
    shaped = product.reshape(n_grp, n_sub, block, kv_width)
    summed = lax.psum_scatter(shaped, "sub", scatter_dimension=1, tiled=True).reshape(
        n_grp, block, kv_width
    )
    current = summed * scale
    grp_index = lax.axis_index("grp")
    levels = n_grp.bit_length() - 1
    for level in range(levels):
        bit_value = grp_index >> level & 1
        paired = current.reshape(-1, 2, block, kv_width)
        first = paired[:, 0]
        second = paired[:, 1]
        keep = jnp.where(bit_value == 0, first, second)
        outgoing = jnp.where(bit_value == 0, second, first)
        received = partner(outgoing, "grp", level)
        lower = jnp.where(bit_value == 0, keep, received)
        upper = jnp.where(bit_value == 0, received, keep)
        partial_value = jnp.stack(
            [jnp.sum(lower * lower), jnp.sum(upper * upper), jnp.sum(lower * upper)]
        )
        totals = node_sums(partial_value, level)
        current = adasum_pair(lower, upper, totals)
    combined = current.reshape(block, kv_width)
    new_momentum = 0.9 * momentum + combined
    new_master = master - 0.05 * new_momentum
    new_weight = lax.all_gather(new_master.astype(jnp.bfloat16), ("grp", "sub"), axis=0, tiled=True)
    return (input_grad, new_momentum, new_master, new_weight)


def solution(mesh):
    return jax.shard_map(
        body,
        mesh=mesh,
        in_specs=(
            P(("grp", "sub"), None),
            P(("grp", "sub"), None),
            P(),
            P(("grp", "sub"), None),
            P(("grp", "sub"), None),
        ),
        out_specs=(P(("grp", "sub"), None), P(("grp", "sub"), None), P(("grp", "sub"), None), P()),
        check_vma=False,
    )
```

profile of v0, /device:TPU:1, one launch (start us, length us, event | category | flops | bytes accessed | tf_op | source)
XLA Modules:
  0.0 353.3 jit_solution(12795257308865639507)
XLA Ops:
  7.2 0.0 copy-start
  7.2 0.0 reduce-scatter.4.cloned.1.call-start
  7.2 1.8 copy-done
  9.1 9.1 %fusion.6 = f32[2048,1024]{1,0:T(8,128)S(1)} fusion(bf16[1536,2048]{1,0:T(8,128)(2,1)} %param.5, bf16[1536,1024]{1,0:T(8,128)(2,1)S(1)} %copy-done), kind=kOutput, calls=%fused_computation.36 | convolution fusion | flops 6442450944 | bytes 17825792 | tf_op jit(solution)/shard_map/dot_general | solution.py:41
  18.2 4.1 %copy.26 = f32[8,16,16,1024]{3,2,0,1:T(8,128)} copy(f32[8,16,16,1024]{3,2,1,0:T(8,128)S(1)} %bitcast.99) | data formatting | bytes 16777216 | tf_op jit(solution)/shard_map/reshape | solution.py:44
  22.2 0.0 reduce-scatter.4.cloned.1.call-update
  22.3 0.0 all-gather.2.cloned.1.call-start
  22.3 87.1 %reduce-scatter.4.cloned.1.call-done = f32[8,1,16,1024]{3,2,0,1:T(8,128)} async-done(((f32[8,16,16,1024]{3,2,0,1:T(8,128)}), f32[8,1,16,1024]{3,2,0,1:T(8,128)}) %reduce-scatter.4.cloned.1.call-update) | async-done | bytes 524304
  109.4 1.1 broadcast_multiply_fusion
  110.5 0.8 copy-done.1
  111.3 0.7 select_bitcast_fusion
  112.0 1.8 collective-permute-start
  113.9 1.4 collective-permute-done
  115.2 2.6 multiply_reduce_fusion.2
  117.8 2.0 pad_maximum_fusion
  119.8 31.2 %psum.21 = f32[3]{0:T(128)S(1)} all-reduce(f32[3]{0:T(128)S(1)} %pad_maximum_fusion), channel_id=1, replica_groups=mesh['grp'=8,'sub'=16] {'sub'}, use_global_device_ids=true, to_apply=%region_4.5 | all-reduce | flops 3 | bytes 24 | tf_op jit(solution)/shard_map/psum | solution.py:16
  151.0 7.4 %collective-permute-start.1 = (f32[3]{0:T(128)S(1)}, f32[3]{0:T(128)S(1)}, u32[]{:S(2)}, u32[]{:S(2)}) collective-permute-start(f32[3]{0:T(128)S(1)} %psum.21), channel_id=1, source_target_pairs={{0,16},{16,0},{32,48},{48,32},{64,80},{80,64},{96,112},{112,96},{1... | collective-permute-start | bytes 44 | tf_op jit(solution)/shard_map/ppermute | solution.py:12
  158.4 0.8 collective-permute-done.1
  159.2 0.6 fusion.5
  162.4 1.1 multiply_add_fusion
  163.5 1.3 collective-permute-start.2
  164.8 3.6 %collective-permute-done.2 = f32[2,16,1024]{2,1,0:T(8,128)} collective-permute-done((f32[2,16,1024]{2,1,0:T(8,128)S(1)}, f32[2,16,1024]{2,1,0:T(8,128)}, u32[]{:S(2)}, u32[]{:S(2)}) %collective-permute-start.2) | collective-permute-done | bytes 131104 | tf_op jit(solution)/shard_map/ppermute | solution.py:12
  168.5 2.2 multiply_reduce_fusion.5
  170.7 2.0 pad_maximum_fusion.1
  172.7 28.5 %psum.22 = f32[3]{0:T(128)S(1)} all-reduce(f32[3]{0:T(128)S(1)} %pad_maximum_fusion.1), channel_id=1, replica_groups=mesh['grp'=8,'sub'=16] {'sub'}, use_global_device_ids=true, to_apply=%region_8.9 | all-reduce | flops 3 | bytes 24 | tf_op jit(solution)/shard_map/psum | solution.py:16
  201.2 8.1 %collective-permute-start.3 = (f32[3]{0:T(128)S(1)}, f32[3]{0:T(128)S(1)}, u32[]{:S(2)}, u32[]{:S(2)}) collective-permute-start(f32[3]{0:T(128)S(1)} %psum.22), channel_id=1, source_target_pairs={{0,16},{16,0},{32,48},{48,32},{64,80},{80,64},{96,112},{112,96},{1... | collective-permute-start | bytes 44 | tf_op jit(solution)/shard_map/ppermute | solution.py:12
  209.3 0.8 collective-permute-done.3
  210.2 1.2 collective-permute-start.4
  211.4 1.1 collective-permute-done.4
  212.6 0.6 fusion.4
  215.8 0.9 add_bitcast_fusion
  216.7 2.9 collective-permute-start.5
  219.6 1.8 collective-permute-done.5
  221.4 0.6 multiply_reduce_fusion.8
  222.0 2.0 pad_maximum_fusion.2
  224.0 30.3 %psum.23 = f32[3]{0:T(128)S(1)} all-reduce(f32[3]{0:T(128)S(1)} %pad_maximum_fusion.2), channel_id=1, replica_groups=mesh['grp'=8,'sub'=16] {'sub'}, use_global_device_ids=true, to_apply=%region_12.13 | all-reduce | flops 3 | bytes 24 | tf_op jit(solution)/shard_map/psum | solution.py:16
  254.3 9.8 %collective-permute-start.6 = (f32[3]{0:T(128)S(1)}, f32[3]{0:T(128)S(1)}, u32[]{:S(2)}, u32[]{:S(2)}) collective-permute-start(f32[3]{0:T(128)S(1)} %psum.23), channel_id=1, source_target_pairs={{0,16},{16,0},{32,48},{48,32},{64,80},{80,64},{96,112},{112,96},{1... | collective-permute-start | bytes 44 | tf_op jit(solution)/shard_map/ppermute | solution.py:12
  264.1 0.8 collective-permute-done.6
  265.0 1.2 collective-permute-start.7
  266.2 1.1 collective-permute-done.7
  267.4 2.8 collective-permute-start.8
  270.2 1.1 collective-permute-done.8
  271.3 0.6 fusion.3
  274.5 1.6 fusion.2
  276.0 0.0 all-gather.2.cloned.1.call-update
  276.0 10.8 %convolution_convert_fusion = bf16[1536,2048]{1,0:T(8,128)(2,1)} fusion(bf16[1536,1024]{1,0:T(8,128)(2,1)S(1)} %copy-done, bf16[2048,1024]{1,0:T(8,128)(2,1)} %param.7), kind=kOutput, calls=%fused_computation | convolution fusion | flops 6445596672 | bytes 13631488 | tf_op jit(solution)/shard_map/dot_general | solution.py:38
  286.8 55.0 %all-gather.2.cloned.1.call-done = bf16[2048,1024]{1,0:T(8,128)(2,1)} async-done(((bf16[16,1024]{1,0:T(8,128)(2,1)}), bf16[2048,1024]{1,0:T(8,128)(2,1)}) %all-gather.2.cloned.1.call-update) | async-done | bytes 4194320 | tf_op jit(solution)/shard_map/all_gather | solution.py:69
  341.8 4.6 %copy.38 = bf16[2048,1024]{1,0:T(8,128)(2,1)} copy(bf16[2048,1024]{1,0:T(8,128)(2,1)} %all-gather.2.cloned.1.call-done) | data formatting | bytes 8388608
  (9 shorter events, 0.1 us)
Async XLA Ops:
  7.2 1.9 copy-start
  7.2 102.2 %reduce-scatter.4.cloned.1.call-start = ((), (), s32[]{:S(2)}) async-start(), calls=%async_computation.2 | async-start | bytes 8912896
  22.3 319.5 %all-gather.2.cloned.1.call-start = ((), (), s32[]{:S(2)}) async-start(), calls=%async_computation.1 | async-start | bytes 4227072 | tf_op jit(solution)/shard_map/all_gather | solution.py:69
  110.5 0.8 copy-start.1
  112.0 3.2 collective-permute-start
  151.0 8.2 %collective-permute-start.1 = (f32[3]{0:T(128)S(1)}, f32[3]{0:T(128)S(1)}, u32[]{:S(2)}, u32[]{:S(2)}) collective-permute-start(f32[3]{0:T(128)S(1)} %psum.21), channel_id=1, source_target_pairs={{0,16},{16,0},{32,48},{48,32},{64,80},{80,64},{96,112},{112,96},{1... | collective-permute-start | bytes 44 | tf_op jit(solution)/shard_map/ppermute | solution.py:12
  163.5 5.0 %collective-permute-start.2 = (f32[2,16,1024]{2,1,0:T(8,128)S(1)}, f32[2,16,1024]{2,1,0:T(8,128)}, u32[]{:S(2)}, u32[]{:S(2)}) collective-permute-start(f32[2,16,1024]{2,1,0:T(8,128)S(1)} %select_bitcast_fusion.1), channel_id=1, source_target_pairs={{0,32},{16,48},{32,0},{48,16},{64,96},{80,112},{96,64},{112,80},{1... | collective-permute-start | bytes 393224 | tf_op jit(solution)/shard_map/ppermute | solution.py:12
  201.2 9.0 %collective-permute-start.3 = (f32[3]{0:T(128)S(1)}, f32[3]{0:T(128)S(1)}, u32[]{:S(2)}, u32[]{:S(2)}) collective-permute-start(f32[3]{0:T(128)S(1)} %psum.22), channel_id=1, source_target_pairs={{0,16},{16,0},{32,48},{48,32},{64,80},{80,64},{96,112},{112,96},{1... | collective-permute-start | bytes 44 | tf_op jit(solution)/shard_map/ppermute | solution.py:12
  210.2 2.4 collective-permute-start.4
  216.7 4.7 %collective-permute-start.5 = (f32[1,16,1024]{2,1,0:T(8,128)S(1)}, f32[1,16,1024]{2,1,0:T(8,128)S(1)}, u32[]{:S(2)}, u32[]{:S(2)}) collective-permute-start(f32[1,16,1024]{2,1,0:T(8,128)S(1)} %select_bitcast_fusion.2), channel_id=1, source_target_pairs={{0,64},{16,80},{32,96},{48,112},{64,0},{80,16},{96,32},{112,48},{1... | collective-permute-start | bytes 196616 | tf_op jit(solution)/shard_map/ppermute | solution.py:12
  254.3 10.7 %collective-permute-start.6 = (f32[3]{0:T(128)S(1)}, f32[3]{0:T(128)S(1)}, u32[]{:S(2)}, u32[]{:S(2)}) collective-permute-start(f32[3]{0:T(128)S(1)} %psum.23), channel_id=1, source_target_pairs={{0,16},{16,0},{32,48},{48,32},{64,80},{80,64},{96,112},{112,96},{1... | collective-permute-start | bytes 44 | tf_op jit(solution)/shard_map/ppermute | solution.py:12
  265.0 2.4 collective-permute-start.7
  267.4 3.9 %collective-permute-start.8 = (f32[3]{0:T(128)S(1)}, f32[3]{0:T(128)S(1)}, u32[]{:S(2)}, u32[]{:S(2)}) collective-permute-start(f32[3]{0:T(128)S(1)} %add.72), channel_id=1, source_target_pairs={{0,64},{16,80},{32,96},{48,112},{64,0},{80,16},{96,32},{112,48},{1... | collective-permute-start | bytes 44 | tf_op jit(solution)/shard_map/ppermute | solution.py:12
Sparse Core Ops, SparseCore 0:
  22.4 86.9 reduce-scatter.3
  276.2 65.5 all-gather.1
where the time goes:
time: 354 us; the launch traced here: 353 us
  waiting for transfers between devices  155 us (44%)
  blocking collectives  90 us (25%)
  starting transfers between devices  36.9 us (10%)
  between operations  21.9 us (6%)
  matrix products  19.9 us (6%)
  other arithmetic  16.8 us (5%)
  local copies, waits for them, and re-layouts  13.1 us (4%)
    psum x3, blocking collectives, node_sums(): totals = lax.psum(partial_value, 'sub')  90 us
    unnamed x3, waiting for transfers between devices  87.1 us
    all_gather x1, waiting for transfers between devices, body(): lax.all_gather(new_master.astype(jnp.bfloat16), ('grp', 'sub'), axis=0, t...  55 us
    ppermute x9, starting transfers between devices, partner(): return lax.ppermute(value, axis, pairs)  36.8 us
    ppermute x9, waiting for transfers between devices, partner(): return lax.ppermute(value, axis, pairs)  12.6 us
    dot_general x1, matrix products, body(): lax.dot_general(cotangent, weight, (((1,), (1,)), ((), ())), preferred_el...  10.8 us
    dot_general x1, matrix products, body(): lax.dot_general(activations, cotangent, (((0,), (0,)), ((), ())), preferr...  9.1 us
    unnamed x5, local copies, waits for them, and re-layouts  7.27 us
  transfers between devices with their start and end apart: 11, of which 11 were waited for; matrix products, arithmetic and copies ran while one was open for 3% of the time, Pallas kernels for 0%

commit v1 on v0

v1 whole, which is shorter than its diff:
```python
import functools
import math

import jax
import jax.numpy as jnp
from jax import lax
from jax.experimental import pallas as pl
from jax.experimental.pallas import tpu as pltpu
from jax.sharding import PartitionSpec as P

MESH = pl.DeviceIdType.MESH
N = 8
LAG2, LAG3, LAG4, LAG5 = 1, 3, 4, 5
PARTS = ((0, 384, "zxy"), (384, 384, "xyz"), (768, 256, "yzx"))
PAIRS = [(i, j) for i in range(N) for j in range(i, N)]


def mod(v, n):
    return lax.rem(v + n, n)


def adasum_coefficients(gram):
    def get(m, i, j):
        return m[(i, j)] if i <= j else m[(j, i)]

    weights = [{i: None} for i in range(N)]
    count = N
    while count > 1:
        half = count // 2
        coef = []
        for i in range(half):
            cross = get(gram, 2 * i, 2 * i + 1)
            lower_sq = jnp.maximum(get(gram, 2 * i, 2 * i), 0.0)
            upper_sq = jnp.maximum(get(gram, 2 * i + 1, 2 * i + 1), 0.0)
            coef.append(
                (
                    1.0 - cross / (2.0 * (lower_sq + 1e-06)),
                    1.0 - cross / (2.0 * (upper_sq + 1e-06)),
                )
            )
        joined = []
        for i in range(half):
            node = {}
            for side in range(2):
                for leaf, w in weights[2 * i + side].items():
                    node[leaf] = coef[i][side] if w is None else w * coef[i][side]
            joined.append(node)
        weights = joined
        new_gram = {}
        for i in range(half):
            for j in range(i, half):
                total = None
                for a in range(2):
                    for b in range(2):
                        term = coef[i][a] * coef[j][b] * get(gram, 2 * i + a, 2 * j + b)
                        total = term if total is None else total + term
                new_gram[(i, j)] = total
        gram = new_gram
        count = half
    return [weights[0][i] for i in range(N)]


def kernel(
    scale,
    a_hbm, c_hbm, w_hbm, master_ref, momentum_ref,
    ig_ref, comb_ref, nw_ref,
    a_buf, c_buf, w_buf, part, r1a, r1b, r2a, r2b, fin, t_buf,
    gram_own, gram_x, gram_y, gram_g,
    load_a, load_c, load_w, rs_send, rs_recv, a2a_send, a2a_recv,
    gr_send, gr_recv, ag_send, ag_recv,
):
    grp = lax.axis_index("grp")
    sub = lax.axis_index("sub")
    z, c = grp // 2, lax.rem(grp, 2)
    y, x = sub // 4, lax.rem(sub, 4)

    def at_x(d):
        return (grp, y * 4 + mod(x + d, 4))

    def at_y(d):
        return (grp, mod(y + d, 4) * 4 + x)

    def at_z(d):
        return (mod(z + d, 4) * 2 + c, sub)

    def at_g(d):
        return (mod(grp + d, N), sub)

    along = {"x": (at_x, x), "y": (at_y, y), "z": (at_z, z)}
    other_core = (z * 2 + (1 - c), sub)

    def load_a_copy(k):
        col = pl.multiple_of(mod(grp + 1 + k, N) * 256, 256)
        return pltpu.make_async_copy(a_hbm.at[:, pl.ds(col, 256)], a_buf.at[k], load_a.at[k])

    def load_w_copy(k):
        return pltpu.make_async_copy(w_hbm.at[pl.ds(k * 256, 256)], w_buf.at[k], load_w.at[k])

    load_c_copy = pltpu.make_async_copy(c_hbm, c_buf, load_c)
    load_a_copy(0).start()
    load_c_copy.start()
    for k in range(1, N):
        load_a_copy(k).start()
    for k in range(N):
        load_w_copy(k).start()

    barrier = pltpu.get_barrier_semaphore()
    peers = [at_x(d) for d in (1, 2, 3)] + [at_y(d) for d in (1, 2, 3)]
    peers += [at_g(d) for d in range(1, N)]
    for peer in peers:
        pl.semaphore_signal(barrier, inc=1, device_id=peer, device_id_type=MESH)

    def remote(src, dst, send_sem, recv_sem, peer):
        return pltpu.make_async_remote_copy(
            src_ref=src, dst_ref=dst, send_sem=send_sem, recv_sem=recv_sem,
            device_id=peer, device_id_type=MESH,
        )

    halves = (
        (at_x, x, at_y, y),
        (at_y, y, at_x, x),
    )

    def rs_copy(stage, h, k, d):
        to1, me1, to2, me2 = halves[h]
        step = 1 if d == 0 else -1
        to = to1 if stage < 2 else to2
        if stage == 0:
            src = part.at[h, k, mod(me1 + 2, 4), pl.ds(2 * d, 2)]
            dst = r1a.at[h, k, d]
        elif stage == 1:
            src = part.at[h, k, mod(me1 + step, 4)]
            dst = r1b.at[h, k, d]
        elif stage == 2:
            src = part.at[h, k, me1, mod(me2 + 2, 4), pl.ds(8 * d, 8)]
            dst = r2a.at[h, k, d]
        else:
            src = part.at[h, k, me1, mod(me2 + step, 4)]
            dst = r2b.at[h, k, d]
        return remote(src, dst, rs_send.at[stage, h, k, d], rs_recv.at[stage, h, k, d], to(step))

    def a2a_copy(k):
        return remote(
            fin.at[k], t_buf.at[grp], a2a_send.at[k], a2a_recv.at[grp], at_g(1 + k)
        )

    def stage1(k):
        for h in range(2):
            for d in range(2):
                rs_copy(0, h, k, d).start()

    def stage2(k):
        for h in range(2):
            to1, me1, to2, me2 = halves[h]
            for d in range(2):
                step = 1 if d == 0 else -1
                rs_copy(0, h, k, d).wait_recv()
                mine = part.at[h, k, mod(me1 + step, 4), pl.ds(2 * d, 2)]
                mine[...] = mine[...] + r1a[h, k, d]
                rs_copy(1, h, k, d).start()

    def stage3(k):
        for h in range(2):
            to1, me1, to2, me2 = halves[h]
            rs_copy(1, h, k, 0).wait_recv()
            rs_copy(1, h, k, 1).wait_recv()
            mine = part.at[h, k, me1]
            mine[...] = mine[...] + (r1b[h, k, 0] + r1b[h, k, 1])
            for d in range(2):
                rs_copy(2, h, k, d).start()

    def stage4(k):
        for h in range(2):
            to1, me1, to2, me2 = halves[h]
            for d in range(2):
                step = 1 if d == 0 else -1
                rs_copy(2, h, k, d).wait_recv()
                mine = part.at[h, k, me1, mod(me2 + step, 4), pl.ds(8 * d, 8)]
                mine[...] = mine[...] + r2a[h, k, d]
                rs_copy(3, h, k, d).start()

    def stage5(k):
        for h in range(2):
            to1, me1, to2, me2 = halves[h]
            rs_copy(3, h, k, 0).wait_recv()
            rs_copy(3, h, k, 1).wait_recv()
            total = part[h, k, me1, me2] + (r2b[h, k, 0] + r2b[h, k, 1])
            fin[k, :, h * 512 : (h + 1) * 512] = total * scale

        @pl.when(k < N - 1)
        def _():
            a2a_copy(k).start()

    def weight_grad(k):
        load_a_copy(k).wait()
        left = a_buf[k]
        for h in range(2):
            res = lax.dot_general(
                left, c_buf[:, h * 512 : (h + 1) * 512],
                (((0,), (0,)), ((), ())), preferred_element_type=jnp.float32,
            )
            for yy in range(4):
                for xx in range(4):
                    row = (yy * 4 + xx) * 16
                    if h == 0:
                        part[h, k, xx, yy] = res[row : row + 16]
                    else:
                        part[h, k, yy, xx] = res[row : row + 16]

    def input_grad(k):
        load_w_copy(k).wait()
        res = lax.dot_general(
            c_buf[...], w_buf[k], (((1,), (1,)), ((), ())), preferred_element_type=jnp.float32
        )
        ig_ref[:, pl.ds(pl.multiple_of(k * 256, 256), 256)] = res.astype(jnp.bfloat16)

    load_c_copy.wait()

    def loop_body(t, carry):
        @pl.when(t < N)
        def _():
            weight_grad(t)

        @pl.when(t == 0)
        def _():
            pl.semaphore_wait(barrier, len(peers))

        @pl.when(t < N)
        def _():
            stage1(t)

        for lag, stage in ((LAG2, stage2), (LAG3, stage3), (LAG4, stage4), (LAG5, stage5)):

            @pl.when((t >= lag) & (t < N + lag))
            def _(lag=lag, stage=stage):
                stage(t - lag)

        @pl.when(t < N)
        def _():
            input_grad(t)

        return carry

    lax.fori_loop(0, N + LAG5, loop_body, 0)

    t_buf[grp] = fin[N - 1]
    for d in range(1, N):
        src = mod(grp + d, N)
        remote(fin.at[0], t_buf.at[src], a2a_send.at[0], a2a_recv.at[src], at_g(d)).wait_recv()

    def fold(v):
        acc = v[:, 0:128]
        for j in range(1, 8):
            acc = acc + v[:, j * 128 : (j + 1) * 128]
        return jnp.sum(acc, axis=0, keepdims=True)

    for n, (i, j) in enumerate(PAIRS):
        gram_own[pl.ds(n, 1), :] = fold(t_buf[i] * t_buf[j])
    gram_own[36:40, :] = jnp.zeros((4, 128), jnp.float32)

    base = 0
    rounds = ((at_x, 3, gram_x), (at_y, 3, gram_y), (at_g, 7, gram_g))
    for r, (to, count, slots) in enumerate(rounds):
        copies = [
            remote(gram_own.at[...] if r == 0 else rounds[r - 1][2].at[rounds[r - 1][1]],
                   slots.at[d - 1], gr_send.at[base + d - 1], gr_recv.at[base + d - 1], to(d))
            for d in range(1, count + 1)
        ]
        for cp in copies:
            cp.start()
        total = gram_own[...] if r == 0 else rounds[r - 1][2][rounds[r - 1][1]]
        for d, cp in enumerate(copies):
            cp.wait_recv()
        for d in range(count):
            total = total + slots[d]
        slots[count] = total
        base += count

    sums = jnp.sum(gram_g[7], axis=1, keepdims=True)
    gram = {pair: sums[n : n + 1, :] for n, pair in enumerate(PAIRS)}
    coef = adasum_coefficients(gram)
    combined = coef[0] * t_buf[0]
    for i in range(1, N):
        combined = combined + coef[i] * t_buf[i]
    comb_ref[...] = combined
    new_master = master_ref[...] - 0.05 * (0.9 * momentum_ref[...] + combined)
    nw_ref[z, c, y, x] = new_master.astype(jnp.bfloat16)

    def ag_region(p, fixed, core):
        col, width, _ = PARTS[p]
        idx = tuple(fixed.get(name, slice(None)) for name in "zyx")
        return nw_ref.at[idx[0], core, idx[1], idx[2], :, pl.ds(col, width)]

    me = {"x": x, "y": y, "z": z}

    def ag_copy(p, s, d, owner_off=0):
        order = PARTS[p][2]
        fixed = {name: mod(me[name] + (owner_off if name == order[s] else 0), 4)
                 for name in order[s:]}
        region = ag_region(p, fixed, c)
        n = (p * 3 + s) * 3 + d - 1
        return remote(region, region, ag_send.at[n], ag_recv.at[n], along[order[s]][0](d))

    def core_copy(p, j, core):
        order = PARTS[p][2]
        region = ag_region(p, {order[2]: mod(me[order[2]] + j, 4)}, core)
        n = 27 + p * 4 + j
        return remote(region, region, ag_send.at[n], ag_recv.at[n], other_core)

    for s in range(3):
        for p in range(3):
            if s > 0:
                for d in range(1, 4):
                    ag_copy(p, s - 1, d, -d).wait_recv()
            for d in range(1, 4):
                ag_copy(p, s, d).start()
            if s == 2:
                core_copy(p, 0, c).start()
    for d in (1, 3, 2):
        for p in range(3):
            ag_copy(p, 2, d, -d).wait_recv()
            core_copy(p, 4 - d, c).start()

    def drain(k, carry):
        for stage in range(4):
            for h in range(2):
                for d in range(2):
                    rs_copy(stage, h, k, d).wait_send()

        @pl.when(k < N - 1)
        def _():
            a2a_copy(k).wait_send()

        return carry

    lax.fori_loop(0, N, drain, 0)
    base = 0
    for r, (to, count, slots) in enumerate(rounds):
        for d in range(1, count + 1):
            remote(gram_own, slots.at[d - 1], gr_send.at[base + d - 1],
                   gr_recv.at[base + d - 1], to(d)).wait_send()
        base += count
    for p in range(3):
        for s in range(3):
            for d in range(1, 4):
                ag_copy(p, s, d).wait_send()
        for j in range(4):
            core_copy(p, j, c).wait_send()
            core_copy(p, j, 1 - c).wait_recv()


def body(activations, cotangent, weight, master, momentum):
    rows, width = activations.shape
    kv = cotangent.shape[1]
    scale = 1.0 / math.sqrt(rows * lax.axis_size("sub"))
    f32, bf16 = jnp.float32, jnp.bfloat16
    dma = pltpu.SemaphoreType.DMA
    vmem = pl.BlockSpec(memory_space=pltpu.VMEM)
    hbm = pl.BlockSpec(memory_space=pl.ANY)
    input_grad, combined, gathered = pl.pallas_call(
        functools.partial(kernel, scale),
        name="fused_step",
        in_specs=[hbm, hbm, hbm, vmem, vmem],
        out_specs=[vmem, vmem, vmem],
        out_shape=[
            pltpu.VMEM((rows, width), bf16),
            pltpu.VMEM((16, kv), f32),
            pltpu.VMEM((4, 2, 4, 4, 16, kv), bf16),
        ],
        scratch_shapes=[
            pltpu.VMEM((N, rows, 256), bf16),
            pltpu.VMEM((rows, kv), bf16),
            pltpu.VMEM((N, 256, kv), bf16),
            pltpu.VMEM((2, N, 4, 4, 16, 512), f32),
            pltpu.VMEM((2, N, 2, 2, 16, 512), f32),
            pltpu.VMEM((2, N, 2, 4, 16, 512), f32),
            pltpu.VMEM((2, N, 2, 8, 512), f32),
            pltpu.VMEM((2, N, 2, 16, 512), f32),
            pltpu.VMEM((N, 16, kv), f32),
            pltpu.VMEM((N, 16, kv), f32),
            pltpu.VMEM((40, 128), f32),
            pltpu.VMEM((4, 40, 128), f32),
            pltpu.VMEM((4, 40, 128), f32),
            pltpu.VMEM((8, 40, 128), f32),
            dma((N,)), dma, dma((N,)),
            dma((4, 2, N, 2)), dma((4, 2, N, 2)),
            dma((N,)), dma((N,)),
            dma((13,)), dma((13,)),
            dma((39,)), dma((39,)),
        ],
        compiler_params=pltpu.CompilerParams(
            collective_id=0, has_side_effects=True, vmem_limit_bytes=46 << 20
        ),
    )(activations, cotangent, weight, master, momentum)
    new_momentum = 0.9 * momentum + combined
    new_master = master - 0.05 * new_momentum
    return (input_grad, new_momentum, new_master, gathered.reshape(width, kv))


def solution(mesh):
    spec = P(("grp", "sub"), None)
    return jax.shard_map(
        body,
        mesh=mesh,
        in_specs=(spec, spec, P(), spec, spec),
        out_specs=(spec, spec, spec, P()),
        check_vma=False,
    )
```

time: 354 us -> 103 us (0.29)
  waiting for transfers between devices: 155 us -> 0 us
  Pallas kernels: 0 us -> 96.7 us
  blocking collectives: 90 us -> 0 us
  starting transfers between devices: 36.9 us -> 0 us
  between operations: 21.9 us -> 0.66 us
  matrix products: 19.9 us -> 0 us
  other arithmetic: 16.8 us -> 0.67 us
  local copies, waits for them, and re-layouts: 13.1 us -> 4.73 us
    pallas_call x0 -> x1, Pallas kernels: none -> 96.7 us  [body(): pl.pallas_call(functools.partial(kernel, scale), name='fused_step', in_sp...]
    psum x3 -> x0, blocking collectives: 90 us -> none  [node_sums(): totals = lax.psum(partial_value, 'sub')]
    unnamed x3 -> x0, waiting for transfers between devices: 87.1 us -> none
    all_gather x1 -> x0, waiting for transfers between devices: 55 us -> none  [body(): lax.all_gather(new_master.astype(jnp.bfloat16), ('grp', 'sub'), axis=0, t...]
    ppermute x9 -> x0, starting transfers between devices: 36.8 us -> none  [partner(): return lax.ppermute(value, axis, pairs)]
    dot_general x2 -> x0, matrix products: 19.9 us -> none  [the longest x1 10.8 us: body(): lax.dot_general(cotangent, weight, (((1,), (1,)), ((), ())), preferred_el...]
    ppermute x9 -> x0, waiting for transfers between devices: 12.6 us -> none  [partner(): return lax.ppermute(value, axis, pairs)]
    another operation x3 -> x0, other arithmetic: 6.01 us -> none  [body(): jnp.stack([jnp.sum(lower * lower), jnp.sum(upper * upper), jnp.sum(lower...]
  transfers between devices with their start and end apart: 11 -> 0, of which waited for: 11 -> 0; matrix products, arithmetic and copies ran while one was open for 3% -> 0% of each run, Pallas kernels for 0% -> 0%
where the time goes in v1:
time: 103 us
  Pallas kernels  96.7 us (94%)
  local copies, waits for them, and re-layouts  4.73 us (5%)
    pallas_call x1, Pallas kernels, body(): pl.pallas_call(functools.partial(kernel, scale), name='fused_step', in_sp...  96.7 us
    unnamed x6, local copies, waits for them, and re-layouts  4.73 us

profile of v1, /device:TPU:1, one launch (start us, length us, event | category | flops | bytes accessed | tf_op | source)
XLA Modules:
  0.0 102.8 jit_solution(16121689750260704969)
XLA Ops:
  0.6 96.7 %fused_step.1 = (bf16[1536,2048]{1,0:T(8,128)(2,1)S(1)}, f32[16,1024]{1,0:T(8,128)S(1)}, bf16[4,2,4,4,16,1024]{5,4,3,2,1,0:T(8,128)(2,1)S(1)}) custom-call(bf16[1536,2048]{1,0:T(8,128)(2,1)} %a_hbm.1, bf16[1536,1024]{1,0:T(8,128)(2,1)} %c_hbm.1, bf16[2048,1024]{1,0:T(8,128)(2,1)} %w_hbm.1, f32[16,1024]{1,0:T(8,128)} %master_ref.1, f32[16,1024]{1,0:T(8,128)} %momentum_ref.1), custom_call_target="tpu_custom_call" | custom-call | tf_op jit(solution)/shard_map/fused_step/pallas_call | solution.py:360
  97.4 0.0 copy-start
  97.4 0.0 copy-start.1
  97.4 2.7 %copy.11 = bf16[1536,2048]{1,0:T(8,128)(2,1)} copy(bf16[1536,2048]{1,0:T(8,128)(2,1)S(1)} %get-tuple-element.12) | data formatting | bytes 12582912
  100.1 0.0 copy-done
  100.1 0.0 copy-done.1
  100.1 0.7 multiply_subtract_fusion
  100.8 2.0 %copy.12 = bf16[2048,1024]{1,0:T(8,128)(2,1)} copy(bf16[2048,1024]{1,0:T(8,128)(2,1)S(1)} %bitcast.1) | data formatting | bytes 8388608
Async XLA Ops:
  97.4 2.7 %copy-start = (f32[16,1024]{1,0:T(8,128)S(1)}, f32[16,1024]{1,0:T(8,128)}, u32[]{:S(2)}) copy-start(f32[16,1024]{1,0:T(8,128)} %master_ref.1) | copy-start | bytes 196612
  97.4 2.7 %copy-start.1 = (f32[16,1024]{1,0:T(8,128)S(1)}, f32[16,1024]{1,0:T(8,128)}, u32[]{:S(2)}) copy-start(f32[16,1024]{1,0:T(8,128)} %momentum_ref.1) | copy-start | bytes 196612

commit v2 on v1

v2 whole, which is shorter than its diff:
```python
import functools
import math

import jax
import jax.numpy as jnp
from jax import lax
from jax.experimental import pallas as pl
from jax.experimental.pallas import tpu as pltpu
from jax.sharding import PartitionSpec as P

MESH = pl.DeviceIdType.MESH
N = 8
LAGS = (0, 2, 4, 6)
SECOND = 6
GRAM = (13, 15, 17, 19)
PARTS = ((0, 384, "yzx"), (384, 384, "xzy"), (768, 256, "xyz"))
PAIRS = [(i, j) for i in range(N) for j in range(i, N)]


def mod(v, n):
    return lax.rem(v + n, n)


def adasum_coefficients(gram):
    def get(m, i, j):
        return m[(i, j)] if i <= j else m[(j, i)]

    weights = [{i: None} for i in range(N)]
    count = N
    while count > 1:
        half = count // 2
        coef = []
        for i in range(half):
            cross = get(gram, 2 * i, 2 * i + 1)
            lower_sq = jnp.maximum(get(gram, 2 * i, 2 * i), 0.0)
            upper_sq = jnp.maximum(get(gram, 2 * i + 1, 2 * i + 1), 0.0)
            coef.append(
                (
                    1.0 - cross / (2.0 * (lower_sq + 1e-06)),
                    1.0 - cross / (2.0 * (upper_sq + 1e-06)),
                )
            )
        joined = []
        for i in range(half):
            node = {}
            for side in range(2):
                for leaf, w in weights[2 * i + side].items():
                    node[leaf] = coef[i][side] if w is None else w * coef[i][side]
            joined.append(node)
        weights = joined
        new_gram = {}
        for i in range(half):
            for j in range(i, half):
                total = None
                for a in range(2):
                    for b in range(2):
                        term = coef[i][a] * coef[j][b] * get(gram, 2 * i + a, 2 * j + b)
                        total = term if total is None else total + term
                new_gram[(i, j)] = total
        gram = new_gram
        count = half
    return [weights[0][i] for i in range(N)]


def kernel(
    scale,
    a_hbm, c_hbm, w_hbm, master_ref, momentum_ref,
    ig_ref, comb_ref, nw0, nw1, nw2,
    a_buf, c_buf, w_buf, part, out, r1a, r1b, r2, fin, t_buf,
    gram_own, gram_x, gram_y, gram_g,
    load_a, load_c, load_w, ring_send, ring_recv, direct_send, direct_recv, a2a_send, a2a_recv,
    gr_send, gr_recv, ag_send, ag_recv,
):
    grp = lax.axis_index("grp")
    sub = lax.axis_index("sub")
    z, c = grp // 2, lax.rem(grp, 2)
    y, x = sub // 4, lax.rem(sub, 4)

    def at_x(d):
        return (grp, y * 4 + mod(x + d, 4))

    def at_y(d):
        return (grp, mod(y + d, 4) * 4 + x)

    def at_z(d):
        return (mod(z + d, 4) * 2 + c, sub)

    def at_g(d):
        return (mod(grp + d, N), sub)

    along = {"x": (at_x, x), "y": (at_y, y), "z": (at_z, z)}
    other_core = (z * 2 + (1 - c), sub)

    def load_a_copy(k):
        col = pl.multiple_of(mod(grp + 1 + k, N) * 256, 256)
        return pltpu.make_async_copy(a_hbm.at[:, pl.ds(col, 256)], a_buf.at[k], load_a.at[k])

    def load_w_copy(k):
        return pltpu.make_async_copy(w_hbm.at[pl.ds(k * 256, 256)], w_buf.at[k], load_w.at[k])

    load_c_copy = pltpu.make_async_copy(c_hbm, c_buf, load_c)
    load_a_copy(0).start()
    load_c_copy.start()
    for k in range(1, N):
        load_a_copy(k).start()
    for k in range(N):
        load_w_copy(k).start()

    barrier = pltpu.get_barrier_semaphore()
    peers = [at_x(d) for d in (1, 2, 3)] + [at_y(d) for d in (1, 2, 3)]
    peers += [at_g(d) for d in range(1, N)]
    for peer in peers:
        pl.semaphore_signal(barrier, inc=1, device_id=peer, device_id_type=MESH)

    def remote(src, dst, send_sem, recv_sem, peer):
        return pltpu.make_async_remote_copy(
            src_ref=src, dst_ref=dst, send_sem=send_sem, recv_sem=recv_sem,
            device_id=peer, device_id_type=MESH,
        )

    halves = (
        (at_x, x, at_y, y),
        (at_y, y, at_x, x),
    )

    def ring_copy(q, stage, h, k, d):
        to1, me1, to2, me2 = halves[h]
        step = 1 if d == 0 else -1
        if stage == 0:
            src = out.at[q, h, k, mod(me1 + 2, 4), pl.ds(2 * d, 2)]
            dst = r1a.at[q, h, k, d]
        else:
            src = out.at[q, h, k, mod(me1 + step, 4)]
            dst = r1b.at[q, h, k, d]
        return remote(
            src, dst, ring_send.at[q, stage, h, k, d], ring_recv.at[q, stage, h, k, d], to1(step)
        )

    def direct_copy(q, h, k, d):
        to1, me1, to2, me2 = halves[h]
        return remote(
            out.at[q, h, k, me1, mod(me2 + d, 4)], r2.at[q, h, k, d - 1],
            direct_send.at[q, h, k, d - 1], direct_recv.at[q, h, k, d - 1], to2(d),
        )

    def a2a_copy(q, k):
        return remote(
            fin.at[q, k], t_buf.at[q, grp], a2a_send.at[q, k], a2a_recv.at[q, grp], at_g(1 + k)
        )

    def put(q, idx, value):
        rounded = value.astype(jnp.bfloat16)
        out[(q,) + idx] = rounded
        if q == 0:
            part[idx] = value - rounded.astype(jnp.float32)

    def wide(v):
        return v.astype(jnp.float32)

    def stage1(q, k):
        for h in range(2):
            to1, me1, to2, me2 = halves[h]
            idx = (h, k, mod(me1 + 2, 4))
            put(q, idx, part[idx])
            for d in range(2):
                ring_copy(q, 0, h, k, d).start()

    def stage2(q, k):
        for h in range(2):
            to1, me1, to2, me2 = halves[h]
            for d in range(2):
                step = 1 if d == 0 else -1
                far = (h, k, mod(me1 + step, 4), pl.ds(2 * (1 - d), 2))
                put(q, far, part[far])
                ring_copy(q, 0, h, k, d).wait_recv()
                near = (h, k, mod(me1 + step, 4), pl.ds(2 * d, 2))
                put(q, near, part[near] + wide(r1a[q, h, k, d]))
                ring_copy(q, 1, h, k, d).start()

    def stage3(q, k):
        for h in range(2):
            to1, me1, to2, me2 = halves[h]
            ring_copy(q, 1, h, k, 0).wait_recv()
            ring_copy(q, 1, h, k, 1).wait_recv()
            part[h, k, me1] = part[h, k, me1] + (wide(r1b[q, h, k, 0]) + wide(r1b[q, h, k, 1]))
            for d in (2, 1, 3):
                idx = (h, k, me1, mod(me2 + d, 4))
                put(q, idx, part[idx])
                direct_copy(q, h, k, d).start()

    def stage4(q, k):
        for h in range(2):
            to1, me1, to2, me2 = halves[h]
            total = part[h, k, me1, me2]
            for d in (1, 3, 2):
                direct_copy(q, h, k, d).wait_recv()
                total = total + wide(r2[q, h, k, d - 1])
            fin[q, k, :, h * 512 : (h + 1) * 512] = total * scale
            if q == 0:
                part[h, k, me1, me2] = jnp.zeros((16, 512), jnp.float32)

        @pl.when(k < N - 1)
        def _():
            a2a_copy(q, k).start()

    def arrived(q):
        t_buf[q, grp] = fin[q, N - 1]
        for d in range(1, N):
            src = mod(grp + d, N)
            remote(
                fin.at[q, 0], t_buf.at[q, src], a2a_send.at[q, 0], a2a_recv.at[q, src], at_g(d)
            ).wait_recv()

    def fold(v):
        acc = v[:, 0:128]
        for j in range(1, 8):
            acc = acc + v[:, j * 128 : (j + 1) * 128]
        return jnp.sum(acc, axis=0, keepdims=True)

    rounds = ((at_x, 3, gram_x), (at_y, 3, gram_y), (at_g, 7, gram_g))
    bases = (0, 3, 6)

    def gram_copy(r, d):
        to, count, slots = rounds[r]
        src = gram_own if r == 0 else rounds[r - 1][2].at[rounds[r - 1][1]]
        n = bases[r] + d - 1
        return remote(src, slots.at[d - 1], gr_send.at[n], gr_recv.at[n], to(d))

    def gram_products():
        arrived(0)
        for n, (i, j) in enumerate(PAIRS):
            gram_own[pl.ds(n, 1), :] = fold(t_buf[0, i] * t_buf[0, j])
        gram_own[36:40, :] = jnp.zeros((4, 128), jnp.float32)

    def gram_start(r):
        for d in range(1, rounds[r][1] + 1):
            gram_copy(r, d).start()

    def gram_sum(r):
        to, count, slots = rounds[r]
        total = gram_own[...] if r == 0 else rounds[r - 1][2][rounds[r - 1][1]]
        for d in range(1, count + 1):
            gram_copy(r, d).wait_recv()
            total = total + slots[d - 1]
        slots[count] = total

    def weight_grad(k):
        load_a_copy(k).wait()
        left = a_buf[k]
        for h in range(2):
            res = lax.dot_general(
                left, c_buf[:, h * 512 : (h + 1) * 512],
                (((0,), (0,)), ((), ())), preferred_element_type=jnp.float32,
            )
            for yy in range(4):
                for xx in range(4):
                    row = (yy * 4 + xx) * 16
                    if h == 0:
                        part[h, k, xx, yy] = res[row : row + 16]
                    else:
                        part[h, k, yy, xx] = res[row : row + 16]

    def input_grad(k):
        load_w_copy(k).wait()
        res = lax.dot_general(
            c_buf[...], w_buf[k], (((1,), (1,)), ((), ())), preferred_element_type=jnp.float32
        )
        ig_ref[:, pl.ds(pl.multiple_of(k * 256, 256), 256)] = res.astype(jnp.bfloat16)

    load_c_copy.wait()

    def loop_body(t, carry):
        @pl.when(t < N)
        def _():
            weight_grad(t)

        @pl.when(t == 0)
        def _():
            pl.semaphore_wait(barrier, len(peers))

        for q in range(2):
            for lag, stage in zip(LAGS, (stage1, stage2, stage3, stage4)):
                first = q * SECOND + lag

                @pl.when((t >= first) & (t < first + N))
                def _(q=q, first=first, stage=stage):
                    stage(q, t - first)

            if q == 0:
                for n, at in enumerate(GRAM):

                    @pl.when(t == at)
                    def _(n=n):
                        if n == 0:
                            gram_products()
                        else:
                            gram_sum(n - 1)
                        if n < 3:
                            gram_start(n)

        @pl.when((t >= N) & (t < 2 * N))
        def _():
            input_grad(t - N)

        return carry

    lax.fori_loop(0, max(SECOND + N + LAGS[3] - 1, GRAM[3]) + 1, loop_body, 0)
    arrived(1)

    sums = jnp.sum(gram_g[7], axis=1, keepdims=True)
    gram = {pair: sums[n : n + 1, :] for n, pair in enumerate(PAIRS)}
    coef = adasum_coefficients(gram)
    combined = coef[0] * (t_buf[0, 0] + t_buf[1, 0])
    for i in range(1, N):
        combined = combined + coef[i] * (t_buf[0, i] + t_buf[1, i])
    comb_ref[...] = combined
    new_master = master_ref[...] - 0.05 * (0.9 * momentum_ref[...] + combined)
    me = {"x": x, "y": y, "z": z}
    gathered = (nw0, nw1, nw2)
    updated = new_master.astype(jnp.bfloat16)
    for p, (col, width, order) in enumerate(PARTS):
        rest = [name for name in "zyx" if name != order[2]]
        gathered[p][c, me[order[2]], me[rest[0]], me[rest[1]]] = updated[:, col : col + width]

    def ag_region(p, fixed, core):
        last = PARTS[p][2][2]
        idx = [fixed.get(name, slice(None)) for name in "zyx" if name != last]
        return gathered[p].at[core, fixed[last], idx[0], idx[1]]

    def hop(p, s, d, back, piece=0):
        order = PARTS[p][2]
        fixed = {name: me[name] for name in order[s:]}
        if s == 2:
            fixed[order[1]] = mod(me[order[1]] + piece, 4)
        if back:
            fixed[order[s]] = mod(me[order[s]] - d, 4)
        region = ag_region(p, fixed, c)
        n = p * 18 + (s + piece) * 3 + d - 1
        return remote(region, region, ag_send.at[n], ag_recv.at[n], along[order[s]][0](d))

    def core_copy(p, j, core):
        order = PARTS[p][2]
        region = ag_region(p, {order[2]: mod(me[order[2]] + j, 4)}, core)
        n = 54 + p * 4 + j
        return remote(region, region, ag_send.at[n], ag_recv.at[n], other_core)

    near_first = (1, 3, 2)
    for p in range(3):
        for d in near_first:
            hop(p, 0, d, False).start()
    for p in range(3):
        for d in near_first:
            hop(p, 0, d, True).wait_recv()
        for d in near_first:
            hop(p, 1, d, False).start()
        for d in near_first:
            hop(p, 2, d, False).start()
    for piece in near_first:
        for p in range(3):
            hop(p, 1, 4 - piece, True).wait_recv()
            for d in near_first:
                hop(p, 2, d, False, piece).start()
    for p in range(3):
        core_copy(p, 0, c).start()
    for d in near_first:
        for p in range(3):
            for piece in range(4):
                hop(p, 2, d, True, piece).wait_recv()
            core_copy(p, 4 - d, c).start()

    def drain(k, carry):
        for q in range(2):
            for h in range(2):
                for d in range(2):
                    for stage in range(2):
                        ring_copy(q, stage, h, k, d).wait_send()
                for d in (1, 2, 3):
                    direct_copy(q, h, k, d).wait_send()

            @pl.when(k < N - 1)
            def _(q=q):
                a2a_copy(q, k).wait_send()

        return carry

    lax.fori_loop(0, N, drain, 0)
    for r in range(3):
        for d in range(1, rounds[r][1] + 1):
            gram_copy(r, d).wait_send()
    for p in range(3):
        for d in near_first:
            hop(p, 0, d, False).wait_send()
            hop(p, 1, d, False).wait_send()
            for piece in range(4):
                hop(p, 2, d, False, piece).wait_send()
        for j in range(4):
            core_copy(p, j, c).wait_send()
            core_copy(p, j, 1 - c).wait_recv()


def write_out(ig_ref, comb_ref, nw0, nw1, nw2, master_ref, momentum_ref,
              ig_out, momentum_out, master_out, nw_out, ig_sems, nw_sems):
    copies = []
    rows = ig_ref.shape[0] // 4
    for i in range(4):
        block = pl.ds(i * rows, rows)
        copies.append(pltpu.make_async_copy(ig_ref.at[block], ig_out.at[block], ig_sems.at[i]))
    for p, ((col, width, order), src) in enumerate(zip(PARTS, (nw0, nw1, nw2))):
        for core in range(2):
            for i in range(4):
                idx = [i if name == order[2] else slice(None) for name in "zyx"]
                dst = nw_out.at[idx[0], core, idx[1], idx[2], :, pl.ds(col, width)]
                copies.append(pltpu.make_async_copy(src.at[core, i], dst, nw_sems.at[p, core, i]))
    for copy in copies:
        copy.start()
    new_momentum = 0.9 * momentum_ref[...] + comb_ref[...]
    momentum_out[...] = new_momentum
    master_out[...] = master_ref[...] - 0.05 * new_momentum
    for copy in copies:
        copy.wait()


def body(activations, cotangent, weight, master, momentum):
    rows, width = activations.shape
    kv = cotangent.shape[1]
    scale = 1.0 / math.sqrt(rows * lax.axis_size("sub"))
    f32, bf16 = jnp.float32, jnp.bfloat16
    dma = pltpu.SemaphoreType.DMA
    vmem = pl.BlockSpec(memory_space=pltpu.VMEM)
    hbm = pl.BlockSpec(memory_space=pl.ANY)
    input_grad, combined, *gathered = pl.pallas_call(
        functools.partial(kernel, scale),
        name="fused_step",
        in_specs=[hbm, hbm, hbm, vmem, vmem],
        out_specs=[vmem] * 5,
        out_shape=[
            pltpu.VMEM((rows, width), bf16),
            pltpu.VMEM((16, kv), f32),
        ]
        + [pltpu.VMEM((2, 4, 4, 4, 16, wide), bf16) for _, wide, _ in PARTS],
        scratch_shapes=[
            pltpu.VMEM((N, rows, 256), bf16),
            pltpu.VMEM((rows, kv), bf16),
            pltpu.VMEM((N, 256, kv), bf16),
            pltpu.VMEM((2, N, 4, 4, 16, 512), f32),
            pltpu.VMEM((2, 2, N, 4, 4, 16, 512), bf16),
            pltpu.VMEM((2, 2, N, 2, 2, 16, 512), bf16),
            pltpu.VMEM((2, 2, N, 2, 4, 16, 512), bf16),
            pltpu.VMEM((2, 2, N, 3, 16, 512), bf16),
            pltpu.VMEM((2, N, 16, kv), f32),
            pltpu.VMEM((2, N, 16, kv), f32),
            pltpu.VMEM((40, 128), f32),
            pltpu.VMEM((4, 40, 128), f32),
            pltpu.VMEM((4, 40, 128), f32),
            pltpu.VMEM((8, 40, 128), f32),
            dma((N,)), dma, dma((N,)),
            dma((2, 2, 2, N, 2)), dma((2, 2, 2, N, 2)),
            dma((2, 2, N, 3)), dma((2, 2, N, 3)),
            dma((2, N)), dma((2, N)),
            dma((13,)), dma((13,)),
            dma((66,)), dma((66,)),
        ],
        compiler_params=pltpu.CompilerParams(
            collective_id=0, has_side_effects=True, vmem_limit_bytes=50 << 20
        ),
    )(activations, cotangent, weight, master, momentum)
    outs = pl.pallas_call(
        write_out,
        name="write_out",
        in_specs=[vmem] * 7,
        out_specs=[hbm, vmem, vmem, hbm],
        out_shape=[
            jax.ShapeDtypeStruct((rows, width), bf16),
            jax.ShapeDtypeStruct((16, kv), f32),
            jax.ShapeDtypeStruct((16, kv), f32),
            jax.ShapeDtypeStruct((4, 2, 4, 4, 16, kv), bf16),
        ],
        scratch_shapes=[dma((4,)), dma((3, 2, 4))],
        compiler_params=pltpu.CompilerParams(vmem_limit_bytes=2 << 20),
    )(input_grad, combined, *gathered, master, momentum)
    return (*outs[:3], outs[3].reshape(width, kv))


def solution(mesh):
    spec = P(("grp", "sub"), None)
    return jax.shard_map(
        body,
        mesh=mesh,
        in_specs=(spec, spec, P(), spec, spec),
        out_specs=(spec, spec, spec, P()),
        check_vma=False,
    )
```

time: 103 us -> 95.6 us (0.928)
  local copies, waits for them, and re-layouts: 4.73 us -> 0.01 us
  Pallas kernels: 96.7 us -> 94.3 us
    pallas_call x1, Pallas kernels: 96.7 us -> 89.5 us  [body(): pl.pallas_call(functools.partial(kernel, scale), name='fused_step', in_sp...]
    pallas_call x0 -> x1, Pallas kernels: none -> 4.8 us  [body(): pl.pallas_call(write_out, name='write_out', in_specs=[vmem] * 7, out_spec...]
    unnamed x6 -> x4, local copies, waits for them, and re-layouts: 4.73 us -> 0.01 us
where the time goes in v2:
time: 95.6 us; the launch traced here: 95 us
  Pallas kernels  94.3 us (99%)
    pallas_call x1, Pallas kernels, body(): pl.pallas_call(functools.partial(kernel, scale), name='fused_step', in_sp...  89.5 us
    pallas_call x1, Pallas kernels, body(): pl.pallas_call(write_out, name='write_out', in_specs=[vmem] * 7, out_spec...  4.8 us

profile of v2, /device:TPU:1, one launch (start us, length us, event | category | flops | bytes accessed | tf_op | source)
XLA Modules:
  0.0 95.0 jit_solution(18394609132709391083)
XLA Ops:
  0.6 0.0 copy-start.1
  0.6 0.0 copy-start
  0.7 89.5 %fused_step.1 = (bf16[1536,2048]{1,0:T(8,128)(2,1)S(1)}, f32[16,1024]{1,0:T(8,128)S(1)}, bf16[2,4,4,4,16,384]{5,4,3,2,1,0:T(8,128)(2,1)S(1)}, bf16[2,4,4,4,16,38...) custom-call(bf16[1536,2048]{1,0:T(8,128)(2,1)} %a_hbm.1, bf16[1536,1024]{1,0:T(8,128)(2,1)} %c_hbm.1, ...), custom_call_target="tpu_custom_call" | custom-call | tf_op jit(solution)/shard_map/fused_step/pallas_call | solution.py:431
  90.2 0.0 copy-done.1
  90.2 0.0 copy-done
  90.2 4.8 %write_out.1 = (bf16[1536,2048]{1,0:T(8,128)(2,1)}, f32[16,1024]{1,0:T(8,128)}, f32[16,1024]{1,0:T(8,128)}, bf16[4,2,4,4,16,1024]{5,4,3,2,1,0:T(8,128)(2,1)}) custom-call(bf16[1536,2048]{1,0:T(8,128)(2,1)S(1)} %get-tuple-element.13.ig_ref, f32[16,1024]{1,0:T(8,128)S(1)} %get-tuple-element.14.comb_ref, ...), custom_call_target="tpu_custom_call" | custom-call | tf_op jit(solution)/shard_map/write_out/pallas_call | solution.py:467
Async XLA Ops:
  0.6 89.6 %copy-start.1 = (f32[16,1024]{1,0:T(8,128)S(1)}, f32[16,1024]{1,0:T(8,128)}, u32[]{:S(2)}) copy-start(f32[16,1024]{1,0:T(8,128)} %momentum_ref.3) | copy-start | bytes 196612
  0.6 89.6 %copy-start = (f32[16,1024]{1,0:T(8,128)S(1)}, f32[16,1024]{1,0:T(8,128)}, u32[]{:S(2)}) copy-start(f32[16,1024]{1,0:T(8,128)} %master_ref.3) | copy-start | bytes 196612

commit v3 on v2

--- a/solution.py
+++ b/solution.py
@@ -101,10 +101,6 @@
     load_c_copy = pltpu.make_async_copy(c_hbm, c_buf, load_c)
     load_a_copy(0).start()
     load_c_copy.start()
-    for k in range(1, N):
-        load_a_copy(k).start()
-    for k in range(N):
-        load_w_copy(k).start()
 
     barrier = pltpu.get_barrier_semaphore()
     peers = [at_x(d) for d in (1, 2, 3)] + [at_y(d) for d in (1, 2, 3)]
@@ -268,6 +264,10 @@
         ig_ref[:, pl.ds(pl.multiple_of(k * 256, 256), 256)] = res.astype(jnp.bfloat16)
 
     load_c_copy.wait()
+    for k in range(1, N):
+        load_a_copy(k).start()
+    for k in range(N):
+        load_w_copy(k).start()
 
     def loop_body(t, carry):
         @pl.when(t < N)
@@ -348,6 +348,27 @@
     for p in range(3):
         for d in near_first:
             hop(p, 0, d, False).start()
+
+    def drain(k, carry):
+        for q in range(2):
+            for h in range(2):
+                for d in range(2):
+                    for stage in range(2):
+                        ring_copy(q, stage, h, k, d).wait_send()
+                for d in (1, 2, 3):
+                    direct_copy(q, h, k, d).wait_send()
+
+            @pl.when(k < N - 1)
+            def _(q=q):
+                a2a_copy(q, k).wait_send()
+
+        return carry
+
+    lax.fori_loop(0, N, drain, 0)
+    for r in range(3):
+        for d in range(1, rounds[r][1] + 1):
+            gram_copy(r, d).wait_send()
+
     for p in range(3):
         for d in near_first:
             hop(p, 0, d, True).wait_recv()
@@ -362,36 +383,19 @@
                 hop(p, 2, d, False, piece).start()
     for p in range(3):
         core_copy(p, 0, c).start()
+        for d in near_first:
+            hop(p, 0, d, False).wait_send()
+            hop(p, 1, d, False).wait_send()
+            hop(p, 2, d, False).wait_send()
     for d in near_first:
         for p in range(3):
             for piece in range(4):
                 hop(p, 2, d, True, piece).wait_recv()
             core_copy(p, 4 - d, c).start()
 
-    def drain(k, carry):
-        for q in range(2):
-            for h in range(2):
-                for d in range(2):
-                    for stage in range(2):
-                        ring_copy(q, stage, h, k, d).wait_send()
-                for d in (1, 2, 3):
-                    direct_copy(q, h, k, d).wait_send()
-
-            @pl.when(k < N - 1)
-            def _(q=q):
-                a2a_copy(q, k).wait_send()
-
-        return carry
-
-    lax.fori_loop(0, N, drain, 0)
-    for r in range(3):
-        for d in range(1, rounds[r][1] + 1):
-            gram_copy(r, d).wait_send()
     for p in range(3):
         for d in near_first:
-            hop(p, 0, d, False).wait_send()
-            hop(p, 1, d, False).wait_send()
-            for piece in range(4):
+            for piece in range(1, 4):
                 hop(p, 2, d, False, piece).wait_send()
         for j in range(4):
             core_copy(p, j, c).wait_send()

time: 95.6 us -> 92.6 us (0.969)
  Pallas kernels: 94.3 us -> 91.8 us
    pallas_call x1, Pallas kernels: 89.5 us -> 87 us  [body(): pl.pallas_call(functools.partial(kernel, scale), name='fused_step', in_sp...]
where the time goes in v3:
time: 92.6 us; the launch traced here: 92.5 us
  Pallas kernels  91.8 us (99%)
    pallas_call x1, Pallas kernels, body(): pl.pallas_call(functools.partial(kernel, scale), name='fused_step', in_sp...  87 us
    pallas_call x1, Pallas kernels, body(): pl.pallas_call(write_out, name='write_out', in_specs=[vmem] * 7, out_spec...  4.8 us

profile of v3, /device:TPU:1, one launch (start us, length us, event | category | flops | bytes accessed | tf_op | source)
XLA Modules:
  0.0 92.5 jit_solution(5017279349129534915)
XLA Ops:
  0.6 0.0 copy-start.1
  0.6 0.0 copy-start
  0.7 87.0 %fused_step.1 = (bf16[1536,2048]{1,0:T(8,128)(2,1)S(1)}, f32[16,1024]{1,0:T(8,128)S(1)}, bf16[2,4,4,4,16,384]{5,4,3,2,1,0:T(8,128)(2,1)S(1)}, bf16[2,4,4,4,16,38...) custom-call(bf16[1536,2048]{1,0:T(8,128)(2,1)} %a_hbm.1, bf16[1536,1024]{1,0:T(8,128)(2,1)} %c_hbm.1, ...), custom_call_target="tpu_custom_call" | custom-call | tf_op jit(solution)/shard_map/fused_step/pallas_call | solution.py:435
  87.7 0.0 copy-done.1
  87.7 0.0 copy-done
  87.7 4.8 %write_out.1 = (bf16[1536,2048]{1,0:T(8,128)(2,1)}, f32[16,1024]{1,0:T(8,128)}, f32[16,1024]{1,0:T(8,128)}, bf16[4,2,4,4,16,1024]{5,4,3,2,1,0:T(8,128)(2,1)}) custom-call(bf16[1536,2048]{1,0:T(8,128)(2,1)S(1)} %get-tuple-element.13.ig_ref, f32[16,1024]{1,0:T(8,128)S(1)} %get-tuple-element.14.comb_ref, ...), custom_call_target="tpu_custom_call" | custom-call | tf_op jit(solution)/shard_map/write_out/pallas_call | solution.py:471
Async XLA Ops:
  0.6 87.0 %copy-start.1 = (f32[16,1024]{1,0:T(8,128)S(1)}, f32[16,1024]{1,0:T(8,128)}, u32[]{:S(2)}) copy-start(f32[16,1024]{1,0:T(8,128)} %momentum_ref.3) | copy-start | bytes 196612
  0.6 87.0 %copy-start = (f32[16,1024]{1,0:T(8,128)S(1)}, f32[16,1024]{1,0:T(8,128)}, u32[]{:S(2)}) copy-start(f32[16,1024]{1,0:T(8,128)} %master_ref.3) | copy-start | bytes 196612

commit v4 on v3

--- a/solution.py
+++ b/solution.py
@@ -338,10 +338,13 @@
         n = p * 18 + (s + piece) * 3 + d - 1
         return remote(region, region, ag_send.at[n], ag_recv.at[n], along[order[s]][0](d))
 
-    def core_copy(p, j, core):
+    def core_copy(p, core, d=0, piece=0):
         order = PARTS[p][2]
-        region = ag_region(p, {order[2]: mod(me[order[2]] + j, 4)}, core)
-        n = 54 + p * 4 + j
+        fixed = {order[2]: mod(me[order[2]] - d, 4)}
+        if d:
+            fixed[order[1]] = mod(me[order[1]] + piece, 4)
+        region = ag_region(p, fixed, core)
+        n = 54 + p * 13 + (piece * 3 + d if d else 0)
         return remote(region, region, ag_send.at[n], ag_recv.at[n], other_core)
 
     near_first = (1, 3, 2)
@@ -382,24 +385,27 @@
             for d in near_first:
                 hop(p, 2, d, False, piece).start()
     for p in range(3):
-        core_copy(p, 0, c).start()
+        core_copy(p, c).start()
         for d in near_first:
             hop(p, 0, d, False).wait_send()
             hop(p, 1, d, False).wait_send()
             hop(p, 2, d, False).wait_send()
-    for d in near_first:
+    for piece in (0,) + near_first:
         for p in range(3):
-            for piece in range(4):
+            for d in near_first:
                 hop(p, 2, d, True, piece).wait_recv()
-            core_copy(p, 4 - d, c).start()
+                core_copy(p, c, d, piece).start()
 
     for p in range(3):
         for d in near_first:
             for piece in range(1, 4):
                 hop(p, 2, d, False, piece).wait_send()
-        for j in range(4):
-            core_copy(p, j, c).wait_send()
-            core_copy(p, j, 1 - c).wait_recv()
+        core_copy(p, c).wait_send()
+        core_copy(p, 1 - c).wait_recv()
+        for d in near_first:
+            for piece in range(4):
+                core_copy(p, c, d, piece).wait_send()
+                core_copy(p, 1 - c, d, piece).wait_recv()
 
 
 def write_out(ig_ref, comb_ref, nw0, nw1, nw2, master_ref, momentum_ref,
@@ -462,7 +468,7 @@
             dma((2, 2, N, 3)), dma((2, 2, N, 3)),
             dma((2, N)), dma((2, N)),
             dma((13,)), dma((13,)),
-            dma((66,)), dma((66,)),
+            dma((93,)), dma((93,)),
         ],
         compiler_params=pltpu.CompilerParams(
             collective_id=0, has_side_effects=True, vmem_limit_bytes=50 << 20

time: 92.6 us -> 92.1 us (level)
  no operation moved by 1% of the time
where the time goes in v4:
time: 92.1 us; the launch traced here: 91.9 us
  Pallas kernels  91.2 us (99%)
    pallas_call x1, Pallas kernels, body(): pl.pallas_call(functools.partial(kernel, scale), name='fused_step', in_sp...  86.4 us
    pallas_call x1, Pallas kernels, body(): pl.pallas_call(write_out, name='write_out', in_specs=[vmem] * 7, out_spec...  4.8 us

profile of v4, /device:TPU:1, one launch (start us, length us, event | category | flops | bytes accessed | tf_op | source)
XLA Modules:
  0.0 91.9 jit_solution(5982952543393274019)
XLA Ops:
  0.6 0.0 copy-start.1
  0.6 0.0 copy-start
  0.7 86.4 %fused_step.1 = (bf16[1536,2048]{1,0:T(8,128)(2,1)S(1)}, f32[16,1024]{1,0:T(8,128)S(1)}, bf16[2,4,4,4,16,384]{5,4,3,2,1,0:T(8,128)(2,1)S(1)}, bf16[2,4,4,4,16,38...) custom-call(bf16[1536,2048]{1,0:T(8,128)(2,1)} %a_hbm.1, bf16[1536,1024]{1,0:T(8,128)(2,1)} %c_hbm.1, ...), custom_call_target="tpu_custom_call" | custom-call | tf_op jit(solution)/shard_map/fused_step/pallas_call | solution.py:441
  87.1 0.0 copy-done.1
  87.1 0.0 copy-done
  87.1 4.8 %write_out.1 = (bf16[1536,2048]{1,0:T(8,128)(2,1)}, f32[16,1024]{1,0:T(8,128)}, f32[16,1024]{1,0:T(8,128)}, bf16[4,2,4,4,16,1024]{5,4,3,2,1,0:T(8,128)(2,1)}) custom-call(bf16[1536,2048]{1,0:T(8,128)(2,1)S(1)} %get-tuple-element.13.ig_ref, f32[16,1024]{1,0:T(8,128)S(1)} %get-tuple-element.14.comb_ref, ...), custom_call_target="tpu_custom_call" | custom-call | tf_op jit(solution)/shard_map/write_out/pallas_call | solution.py:477
Async XLA Ops:
  0.6 86.5 %copy-start.1 = (f32[16,1024]{1,0:T(8,128)S(1)}, f32[16,1024]{1,0:T(8,128)}, u32[]{:S(2)}) copy-start(f32[16,1024]{1,0:T(8,128)} %momentum_ref.3) | copy-start | bytes 196612
  0.6 86.5 %copy-start = (f32[16,1024]{1,0:T(8,128)S(1)}, f32[16,1024]{1,0:T(8,128)}, u32[]{:S(2)}) copy-start(f32[16,1024]{1,0:T(8,128)} %master_ref.3) | copy-start | bytes 196612
